TPU v7x, 512 devices: a whole 4x4x16 slice. The times are simulated.
512 devices in a mesh: shot: 4 (over x_lo, core), slab: 128 (over z, y, x_hi).
Axes of the slice: x: 4 (x_hi: 2, x_lo: 2; x = x_hi * 2 + x_lo), y: 4, z: 16, core: 2. Of those that a mesh axis runs over, the one named last changes fastest.
Arguments:
- lame_lambda: float32 [256, 32, 128], P('slab'), may hold values from 0.5 to 1.5
- lame_mu: float32 [256, 32, 128], P('slab'), may hold values from 0.3 to 0.8
- buoyancy: float32 [256, 32, 128], P('slab'), may hold values from 0.5 to 1
- forward_state: float32 [4, 9, 256, 32, 128], P('shot', None, 'slab'), may hold values from -6 to 6
- adjoint_state: float32 [4, 9, 256, 32, 128], P('shot', None, 'slab'), may hold values from -6 to 6
- source_wavelet: float32 [4, 8], P('shot'), may hold values from -20 to 20
- source_cell: int32 [4], P('shot'), may hold values from 0 to 1048575
- residual_traces: float32 [4, 8, 16384], P('shot', None, 'slab'), may hold values from -12 to 12
- receiver_slab: int32 [16384, 1], P('slab'), may hold values from 0 to 127; in each aligned block of 128 rows (0 to 127, 128 to 255, ...) at most 2 rows name the same one
- receiver_cell: int32 [16384], P('slab'), may hold values from 0 to 8191
Outputs:
- adjoint_start: float32 [4, 9, 256, 32, 128], P('shot', None, 'slab')
- lambda_gradient: float32 [256, 32, 128], P('slab', 'shot')
- mu_gradient: float32 [256, 32, 128], P('slab', 'shot')
Inputs may be any that keep to these rules, and one draw needn't show every extreme that they name: `receiver_slab`: among the 128 receivers held by one index of slab, at most 2 lie in any one slab.
All inputs are finite; a program needn't handle non-finite values.
Results may differ from a plain program's by a relative error of at most 0.000067.
Values sent between devices are 32-bit elements; how exact they have to be, the bound alone decides.
No kernel may reach another device: no remote copies, remote signals or barrier semaphores. Data moves between devices by JAX's collectives and lax.ppermute only.
A program may use at most 64 MiB of HBM per device.

v0:
```python
import jax
import jax.numpy as jnp
from jax import lax
from jax.sharding import PartitionSpec as P

TIME_STEP = 0.3


def from_behind(value, axis, steps):
    count = lax.axis_size(axis)
    initial, last = (max(0, -steps), min(count, count - steps))
    return lax.ppermute(value, axis, [(source, source + steps) for source in range(initial, last)])


def next_cell(values, along):
    extent = values.shape[along]
    remainder = lax.slice_in_dim(values, 1, extent, axis=along)
    border = jnp.zeros_like(lax.slice_in_dim(values, 0, 1, axis=along))
    return jnp.concatenate([remainder, border], axis=along)


def prev_cell(values, along):
    extent = values.shape[along]
    remainder = lax.slice_in_dim(values, 0, extent - 1, axis=along)
    border = jnp.zeros_like(lax.slice_in_dim(values, 0, 1, axis=along))
    return jnp.concatenate([border, remainder], axis=along)


def velocity_update(velocity, stress, buoyancy, normal_after, shear_before):
    sigma_xx = stress[:, 0]
    sigma_yy = stress[:, 1]
    sigma_zz = stress[:, 2]
    sigma_xy = stress[:, 3]
    sigma_xz = stress[:, 4]
    sigma_yz = stress[:, 5]
    accel_x = (
        normal_after
        - sigma_xx
        + (sigma_xy - prev_cell(sigma_xy, 2))
        + (sigma_xz - prev_cell(sigma_xz, 3))
    )
    accel_y = (
        sigma_xy
        - shear_before[:, 0]
        + (next_cell(sigma_yy, 2) - sigma_yy)
        + (sigma_yz - prev_cell(sigma_yz, 3))
    )
    accel_z = (
        sigma_xz
        - shear_before[:, 1]
        + (sigma_yz - prev_cell(sigma_yz, 2))
        + (next_cell(sigma_zz, 3) - sigma_zz)
    )
    factor = TIME_STEP * buoyancy
    return jnp.stack(
        [
            velocity[:, 0] - factor * accel_x,
            velocity[:, 1] - factor * accel_y,
            velocity[:, 2] - factor * accel_z,
        ],
        axis=1,
    )


def stress_update(velocity, stress, lame_lambda, lame_mu, speed_before, speeds_after):
    speed_x = velocity[:, 0]
    speed_y = velocity[:, 1]
    speed_z = velocity[:, 2]
    strain_xx = speed_x - speed_before[:, 0]
    strain_yy = speed_y - prev_cell(speed_y, 2)
    strain_zz = speed_z - prev_cell(speed_z, 3)
    strain_xy = next_cell(speed_x, 2) - speed_x + (speeds_after[:, 0] - speed_y)
    strain_xz = next_cell(speed_x, 3) - speed_x + (speeds_after[:, 1] - speed_z)
    strain_yz = next_cell(speed_y, 3) - speed_y + (next_cell(speed_z, 2) - speed_z)
    dilation = strain_xx + strain_yy + strain_zz
    volume_term = lame_lambda * dilation
    twice_mu = 2.0 * lame_mu
    updated = jnp.stack(
        [
            stress[:, 0] - TIME_STEP * (volume_term + twice_mu * strain_xx),
            stress[:, 1] - TIME_STEP * (volume_term + twice_mu * strain_yy),
            stress[:, 2] - TIME_STEP * (volume_term + twice_mu * strain_zz),
            stress[:, 3] - TIME_STEP * (lame_mu * strain_xy),
            stress[:, 4] - TIME_STEP * (lame_mu * strain_xz),
            stress[:, 5] - TIME_STEP * (lame_mu * strain_yz),
        ],
        axis=1,
    )
    return (updated, (strain_xx, strain_yy, strain_zz, strain_xy, strain_xz, strain_yz))


def imaging(strains):
    strain_xx, strain_yy, strain_zz, strain_xy, strain_xz, strain_yz = strains
    dilation = strain_xx + strain_yy + strain_zz
    lambda_term = TIME_STEP * (dilation[0] * dilation[1])
    shear_term = 2.0 * (
        strain_xx[0] * strain_xx[1] + strain_yy[0] * strain_yy[1] + strain_zz[0] * strain_zz[1]
    )
    shear_term = (
        shear_term
        + strain_xy[0] * strain_xy[1]
        + strain_xz[0] * strain_xz[1]
        + strain_yz[0] * strain_yz[1]
    )
    return (lambda_term, TIME_STEP * shear_term)


def shards(
    lame_lambda,
    lame_mu,
    buoyancy,
    forward_state,
    adjoint_state,
    source_wavelet,
    source_cell,
    residual_traces,
    receiver_slab,
    receiver_cell,
):
    planes, rows_y, depth = lame_lambda.shape
    cell_count = planes * rows_y * depth
    steps_total = source_wavelet.shape[1]
    my_slab = lax.axis_index("slab")
    traces = residual_traces[0]
    target_slab = receiver_slab[:, 0]
    targets = (target_slab * cell_count + receiver_cell).astype(jnp.float32)[None, :]
    arrived, landing = (
        lax.all_gather(traces, "slab", axis=1, tiled=True),
        lax.all_gather(targets, "slab", axis=1, tiled=True),
    )
    local_cell = landing[0].astype(jnp.int32) - my_slab * cell_count
    usable = (local_cell >= 0) & (local_cell < cell_count)
    cell_index = jnp.where(usable, local_cell, 0)
    amounts = jnp.where(usable[None, :], arrived, 0.0)
    receiver_push = jnp.zeros((steps_total, cell_count), jnp.float32).at[:, cell_index].add(amounts)
    receiver_push = receiver_push.reshape(steps_total, planes, rows_y, depth)
    source_local = source_cell[0] - my_slab * cell_count
    source_spot = (
        (jnp.arange(cell_count, dtype=jnp.int32) == source_local)
        .astype(jnp.float32)
        .reshape(planes, rows_y, depth)
    )
    wavefields = jnp.concatenate([forward_state, adjoint_state], axis=0)
    grad_lambda = jnp.zeros((planes, rows_y, depth), jnp.float32)
    grad_shear = jnp.zeros((planes, rows_y, depth), jnp.float32)
    for step_index in range(steps_total):
        stress_now = wavefields[:, 3:9]
        normal_next = from_behind(stress_now[:, 0, 0:1], "slab", -1)
        shear_prev = from_behind(stress_now[:, 3:5, planes - 1 : planes], "slab", 1)
        normal_after = jnp.concatenate([stress_now[:, 0, 1:], normal_next], axis=1)
        shear_before = jnp.concatenate([shear_prev, stress_now[:, 3:5, : planes - 1]], axis=2)
        velocity = velocity_update(
            wavefields[:, 0:3], stress_now, buoyancy, normal_after, shear_before
        )
        speed_prev = from_behind(velocity[:, 0:1, planes - 1 : planes], "slab", 1)
        speed_next = from_behind(velocity[:, 1:3, 0:1], "slab", -1)
        speed_before = jnp.concatenate([speed_prev, velocity[:, 0:1, : planes - 1]], axis=2)
        speeds_after = jnp.concatenate([velocity[:, 1:3, 1:], speed_next], axis=2)
        stress, strains = stress_update(
            velocity, stress_now, lame_lambda, lame_mu, speed_before, speeds_after
        )
        lambda_term, shear_term = imaging(strains)
        grad_lambda = grad_lambda + lambda_term
        grad_shear = grad_shear + shear_term
        pushes = jnp.stack([source_spot * source_wavelet[0, step_index], receiver_push[step_index]])
        stress = stress.at[:, 0:3].add(-TIME_STEP * pushes[:, None])
        wavefields = jnp.concatenate([velocity, stress], axis=1)
    lambda_part, shear_part = (
        lax.psum_scatter(grad_lambda, "shot", scatter_dimension=1, tiled=True),
        lax.psum_scatter(grad_shear, "shot", scatter_dimension=1, tiled=True),
    )
    return (wavefields[1:2], lambda_part, shear_part)


def solution(mesh):
    in_specs = (
        P("slab", None, None),
        P("slab", None, None),
        P("slab", None, None),
        P("shot", None, "slab", None, None),
        P("shot", None, "slab", None, None),
        P("shot", None),
        P("shot"),
        P("shot", None, "slab"),
        P("slab", None),
        P("slab"),
    )
    out_specs = (
        P("shot", None, "slab", None, None),
        P("slab", "shot", None),
        P("slab", "shot", None),
    )
    return jax.shard_map(shards, mesh=mesh, in_specs=in_specs, out_specs=out_specs, check_vma=False)
```

profile of v0, /device:TPU:1, one launch (start us, length us, event | category | flops | bytes accessed | tf_op | source)
XLA Modules:
  0.0 1153.6 jit_solution(3995360313206360715)
XLA Ops:
  7.2 0.8 fusion.81
  8.0 5.5 collective-permute-start.2
  13.5 0.8 fusion.298
  14.3 1.3 collective-permute-start
  15.6 0.9 fusion.83
  16.5 0.8 broadcast_multiply_fusion.2
  17.3 0.8 broadcast_multiply_fusion.1
  18.1 1.6 fusion.335
  21.1 304.9 %all-gather.2 = f32[128,1,128]{2,1,0:T(1,128)S(1)} all-gather(f32[1,1,128]{2,1,0:T(1,128)S(1)} %fusion.300), channel_id=2, replica_groups=mesh['shot'=4,'slab'=128] {'slab'}, dimensions={0}, use_global_device_ids=true | all-gather | bytes 66048 | tf_op jit(solution)/shard_map/all_gather | solution.py:129
  326.0 294.9 %all-gather.1 = f32[1,8,16384]{2,1,0:T(8,128)S(1)} all-gather(f32[1,8,128]{2,1,0:T(8,128)} %param.33), channel_id=3, replica_groups=mesh['shot'=4,'slab'=128] {'slab'}, dimensions={2}, use_global_device_ids=true | all-gather | bytes 528384 | tf_op jit(solution)/shard_map/all_gather | solution.py:128
  620.9 5.3 copy.267
  626.3 115.0 %scatter_custom_fusion = f32[8,8192]{0,1:T(8,128)} fusion(s32[16384]{0:T(1024)S(1)} %bitcast.957, f32[16384,8]{1,0:T(8,128)} %copy.267, f32[]{:T(128)} %constant.207.clone.1), kind=kCustom, calls=%fused_computation.9 | custom fusion | flops 131072 | bytes 262656 | tf_op jit(solution)/shard_map/scatter-add | solution.py:135
  741.3 28.7 %slice_reduce_fusion = (f32[8192]{0:T(1024)}, f32[8192]{0:T(1024)S(1)}, f32[8192]{0:T(1024)S(1)}, f32[8192]{0:T(1024)S(1)}, f32[8192]{0:T(1024)S(1)}, /*index=5*...) fusion(f32[8,8192]{0,1:T(8,128)} %scatter_custom_fusion), kind=kLoop, calls=%fused_computation.1 | loop fusion | bytes 524288 | tf_op jit(solution)/shard_map/slice | solution.py:165
  770.6 1.3 broadcast_select_fusion.6
  771.9 1.3 broadcast_select_fusion.4
  773.2 1.3 broadcast_select_fusion.2
  774.8 5.1 collective-permute-start.1
  780.2 1.3 collective-permute-start.4
  782.2 1.3 collective-permute-start.3
  783.6 3.0 collective-permute-done.4
  786.8 3.1 collective-permute-start.6
  790.1 5.8 collective-permute-start.5
  796.1 1.3 collective-permute-start.8
  797.5 5.2 collective-permute-done.8
  802.9 1.3 collective-permute-start.7
  804.3 5.5 collective-permute-start.10
  810.0 3.7 collective-permute-start.9
  814.0 1.3 collective-permute-start.12
  815.3 5.2 collective-permute-done.12
  820.7 1.3 collective-permute-start.11
  822.1 5.5 collective-permute-start.14
  827.8 5.2 collective-permute-start.13
  833.3 1.3 collective-permute-start.16
  834.7 5.2 collective-permute-done.16
  840.0 1.3 collective-permute-start.15
  841.4 5.5 collective-permute-start.18
  847.1 3.7 collective-permute-start.17
  851.0 1.3 collective-permute-start.20
  853.1 4.3 collective-permute-done.20
  857.5 0.7 multiply_multiply_fusion.1
  858.4 4.3 collective-permute-start.22
  863.5 1.3 collective-permute-start.19
  864.8 4.8 collective-permute-done.19
  869.8 1.3 collective-permute-start.24
  871.1 5.7 collective-permute-start.21
  877.7 0.8 multiply_subtract_fusion.4
  878.6 5.1 collective-permute-start.26
  883.8 1.3 collective-permute-start.23
  885.1 5.6 collective-permute-done.23
  891.0 1.3 collective-permute-start.28
  892.3 6.4 collective-permute-start.25
  899.7 0.8 multiply_subtract_fusion.1
  900.5 1.3 collective-permute-start.27
  901.9 6.4 collective-permute-start.29
  909.8 6.0 collective-permute-start.30
  918.0 1.3 collective-permute-start.31
  921.4 3.8 collective-permute-done.31
  925.2 0.9 bitcast_dynamic-update-slice_fusion.2
  926.1 0.9 bitcast_dynamic-update-slice_fusion.1
  927.0 0.9 bitcast_dynamic-update-slice_fusion
  927.9 2.1 fusion.241
  930.1 0.7 fusion.3
  930.8 187.0 %reduce-scatter.3.cloned.1.call-done = f32[2,8,128]{2,1,0:T(8,128)} async-done(((f32[2,32,128]{2,1,0:T(8,128)}), f32[2,8,128]{2,1,0:T(8,128)}) %reduce-scatter.3.cloned.1.call-update) | async-done | bytes 8208 | tf_op jit(solution)/shard_map/reduce_scatter | solution.py:169
  1117.9 28.9 %reduce-scatter.5.cloned.1.call-done = f32[2,8,128]{2,1,0:T(8,128)} async-done(((f32[2,32,128]{2,1,0:T(8,128)}), f32[2,8,128]{2,1,0:T(8,128)}) %reduce-scatter.5.cloned.1.call-update) | async-done | bytes 8208 | tf_op jit(solution)/shard_map/reduce_scatter | solution.py:170
  (193 shorter events, 15.4 us)
Async XLA Ops:
  7.2 1110.7 %reduce-scatter.3.cloned.1.call-start = ((), (), s32[]{:S(2)}) async-start(), calls=%async_computation.2 | async-start | bytes 40960 | tf_op jit(solution)/shard_map/reduce_scatter | solution.py:169
  8.0 766.5 %collective-permute-start.2 = (f32[2,2,1,32,128]{4,3,0,2,1:T(8,128)S(1)}, f32[2,2,1,32,128]{4,3,0,2,1:T(8,128)S(1)}, u32[]{:S(2)}, u32[]{:S(2)}) collective-permute-start(f32[2,2,1,32,128]{4,3,0,2,1:T(8,128)S(1)} %get-tuple-element.218), channel_id=1, source_target_pairs={{0,1},{1,2},{2,3},{3,4},{4,5},{5,6},{6,7},{7,8},{8,9},{9,10},{10,1... | collective-permute-start | bytes 196616 | tf_op jit(solution)/shard_map/ppermute | solution.py:12
  14.3 760.4 %collective-permute-start = (f32[2,1,32,128]{3,2,0,1:T(8,128)S(1)}, f32[2,1,32,128]{3,2,0,1:T(8,128)S(1)}, u32[]{:S(2)}, u32[]{:S(2)}) collective-permute-start(f32[2,1,32,128]{3,2,0,1:T(8,128)S(1)} %get-tuple-element.213), channel_id=1, source_target_pairs={{1,0},{2,1},{3,2},{4,3},{5,4},{6,5},{7,6},{8,7},{9,8},{10,9},{11,1... | collective-permute-start | bytes 98312 | tf_op jit(solution)/shard_map/ppermute | solution.py:12
  741.3 33.2 %copy-start = (f32[1,9,2,32,128]{4,3,2,1,0:T(8,128)S(1)}, f32[1,9,2,32,128]{4,3,2,1,0:T(8,128)}, u32[]{:S(2)}) copy-start(f32[1,9,2,32,128]{4,3,2,1,0:T(8,128)} %param.29) | copy-start | bytes 884740
  741.3 33.2 %copy-start.1 = (f32[1,9,2,32,128]{4,3,2,1,0:T(8,128)S(1)}, f32[1,9,2,32,128]{4,3,2,1,0:T(8,128)}, u32[]{:S(2)}) copy-start(f32[1,9,2,32,128]{4,3,2,1,0:T(8,128)} %param.30) | copy-start | bytes 884740
  770.0 11.5 copy-start.2
  770.0 16.7 %copy-start.3 = (f32[2,32,128]{2,1,0:T(8,128)S(1)}, f32[2,32,128]{2,1,0:T(8,128)}, u32[]{:S(2)}) copy-start(f32[2,32,128]{2,1,0:T(8,128)} %param.27) | copy-start | bytes 98308
  774.8 6.6 collective-permute-start.1
  780.2 6.5 collective-permute-start.4
  782.2 7.6 collective-permute-start.3
  786.8 9.1 collective-permute-start.6
  790.1 7.4 collective-permute-start.5
  796.1 6.5 collective-permute-start.8
  802.9 6.9 collective-permute-start.7
  804.3 9.4 collective-permute-start.10
  810.0 5.3 collective-permute-start.9
  814.0 6.5 collective-permute-start.12
  820.7 6.9 collective-permute-start.11
  822.1 11.0 collective-permute-start.14
  827.8 6.8 collective-permute-start.13
  833.3 6.5 collective-permute-start.16
  840.0 6.9 collective-permute-start.15
  841.4 9.4 collective-permute-start.18
  847.1 6.1 collective-permute-start.17
  850.8 26.0 %copy-start.7 = (f32[8192]{0:T(1024)S(1)}, f32[8192]{0:T(1024)}, u32[]{:S(2)}) copy-start(f32[8192]{0:T(1024)} %get-tuple-element.108) | copy-start | bytes 98308
  851.0 6.5 collective-permute-start.20
  858.4 6.4 collective-permute-start.22
  863.5 6.2 collective-permute-start.19
  869.8 7.9 collective-permute-start.24
  871.1 6.6 collective-permute-start.21
  878.6 6.5 collective-permute-start.26
  883.8 6.9 collective-permute-start.23
  891.0 8.7 collective-permute-start.28
  892.3 7.4 collective-permute-start.25
  900.5 7.8 collective-permute-start.27
  901.9 14.0 %collective-permute-start.29 = (f32[2,2,1,32,128]{4,3,2,0,1:T(8,128)S(1)}, f32[2,2,1,32,128]{4,3,2,0,1:T(8,128)S(1)}, u32[]{:S(2)}, u32[]{:S(2)}) collective-permute-start(f32[2,2,1,32,128]{4,3,2,0,1:T(8,128)S(1)} %fusion.17), channel_id=1, source_target_pairs={{0,1},{1,2},{2,3},{3,4},{4,5},{5,6},{6,7},{7,8},{8,9},{9,10},{10,1... | collective-permute-start | bytes 196616 | tf_op jit(solution)/shard_map/ppermute | solution.py:12
  909.8 9.5 collective-permute-start.30
  918.0 7.2 collective-permute-start.31
  920.1 226.7 %reduce-scatter.5.cloned.1.call-start = ((), (), s32[]{:S(2)}) async-start(), calls=%async_computation.3 | async-start | bytes 40960 | tf_op jit(solution)/shard_map/reduce_scatter | solution.py:170
  921.4 8.6 copy-start.4
  921.4 8.6 copy-start.5
  921.4 8.6 copy-start.6
Sparse Core Ops, SparseCore 0:
  920.2 197.6 reduce-scatter.2
  1121.4 25.3 reduce-scatter.4
where the time goes:
time: 1160 us; the launch traced here: 1150 us
  blocking collectives  600 us (52%)
  waiting for transfers between devices  253 us (22%)
  other arithmetic  141 us (12%)
  starting transfers between devices  103 us (9%)
  local copies, waits for them, and re-layouts  40.4 us (3%)
  between operations  16 us (1%)
    all_gather x1, blocking collectives, shards(): lax.all_gather(targets, 'slab', axis=1, tiled=True)  305 us
    all_gather x1, blocking collectives, shards(): lax.all_gather(traces, 'slab', axis=1, tiled=True)  295 us
    reduce_scatter x1, waiting for transfers between devices, shards(): lax.psum_scatter(grad_lambda, 'shot', scatter_dimension=1, tiled=True)  187 us
    scatter-add x1, other arithmetic, shards(): jnp.zeros((steps_total, cell_count), jnp.float32).at[:, cell_index]  115 us
    ppermute x32, starting transfers between devices, from_behind(): lax.ppermute(value, axis, [(source, source + steps) for source in range(i...  103 us
    ppermute x32, waiting for transfers between devices, from_behind(): lax.ppermute(value, axis, [(source, source + steps) for source in range(i...  37.4 us
    reduce_scatter x1, waiting for transfers between devices, shards(): lax.psum_scatter(grad_shear, 'shot', scatter_dimension=1, tiled=True)  28.9 us
    slice x1, local copies, waits for them, and re-layouts, shards(): receiver_push[step_index]  28.7 us
  transfers between devices with their start and end apart: 34, of which 11 were waited for; matrix products, arithmetic and copies ran while one was open for 15% of the time, Pallas kernels for 0%

commit v1 on v0

--- a/solution.py
+++ b/solution.py
@@ -4,6 +4,11 @@
 from jax.sharding import PartitionSpec as P
 
 TIME_STEP = 0.3
+
+
+def all_by_exchange(x, axis, dim):
+    stack = jnp.stack([x] * lax.axis_size(axis))
+    return jnp.concatenate(lax.all_to_all(stack, axis, 0, 0), axis=dim)
 
 
 def from_behind(value, axis, steps):
@@ -126,7 +131,7 @@
     targets = (target_slab * cell_count + receiver_cell).astype(jnp.float32)[None, :]
     arrived, landing = (
         lax.all_gather(traces, "slab", axis=1, tiled=True),
-        lax.all_gather(targets, "slab", axis=1, tiled=True),
+        all_by_exchange(targets, "slab", 1),
     )
     local_cell = landing[0].astype(jnp.int32) - my_slab * cell_count
     usable = (local_cell >= 0) & (local_cell < cell_count)

time: 1160 us -> 837 us (0.72)
  blocking collectives: 600 us -> 302 us
  waiting for transfers between devices: 253 us -> 207 us
  starting transfers between devices: 103 us -> 125 us
    all_gather x1 -> x0, blocking collectives: 305 us -> none  [shards(): lax.all_gather(targets, 'slab', axis=1, tiled=True)]
    reduce_scatter x1, waiting for transfers between devices: 187 us -> 136 us  [shards(): lax.psum_scatter(grad_lambda, 'shot', scatter_dimension=1, tiled=True)]
    all_to_all x0 -> x1, starting transfers between devices: none -> 23 us  [all_by_exchange(): return jnp.concatenate(lax.all_to_all(stack, axis, 0, 0), axis=dim)]
  transfers between devices with their start and end apart: 34 -> 35, of which waited for: 11 -> 14; matrix products, arithmetic and copies ran while one was open for 15% -> 4% of each run, Pallas kernels for 0% -> 0%
where the time goes in v1:
time: 837 us; the launch traced here: 835 us
  blocking collectives  302 us (36%)
  waiting for transfers between devices  207 us (25%)
  other arithmetic  144 us (17%)
  starting transfers between devices  125 us (15%)
  local copies, waits for them, and re-layouts  41.2 us (5%)
  between operations  16 us (2%)
    all_gather x1, blocking collectives, shards(): lax.all_gather(traces, 'slab', axis=1, tiled=True)  302 us
    reduce_scatter x1, waiting for transfers between devices, shards(): lax.psum_scatter(grad_lambda, 'shot', scatter_dimension=1, tiled=True)  136 us
    scatter-add x1, other arithmetic, shards(): jnp.zeros((steps_total, cell_count), jnp.float32).at[:, cell_index]  115 us
    ppermute x32, starting transfers between devices, from_behind(): lax.ppermute(value, axis, [(source, source + steps) for source in range(i...  102 us
    ppermute x32, waiting for transfers between devices, from_behind(): lax.ppermute(value, axis, [(source, source + steps) for source in range(i...  41.5 us
    reduce_scatter x1, waiting for transfers between devices, shards(): lax.psum_scatter(grad_shear, 'shot', scatter_dimension=1, tiled=True)  28.9 us
    slice x1, local copies, waits for them, and re-layouts, shards(): receiver_push[step_index]  28.8 us
    all_to_all x1, starting transfers between devices, all_by_exchange(): return jnp.concatenate(lax.all_to_all(stack, axis, 0, 0), axis=dim)  23 us
  transfers between devices with their start and end apart: 35, of which 14 were waited for; matrix products, arithmetic and copies ran while one was open for 4% of the time, Pallas kernels for 0%

profile of v1, /device:TPU:1, one launch (start us, length us, event | category | flops | bytes accessed | tf_op | source)
XLA Modules:
  0.0 835.4 jit_solution(13918147381872450882)
XLA Ops:
  7.2 0.9 fusion.81
  8.1 5.5 collective-permute-start.2
  14.4 1.3 collective-permute-start
  17.0 23.0 %all-to-all-start = ((f32[128,1,128]{2,1,0:T(1,128)}), f32[128,1,128]{2,1,0:T(1,128)S(1)}, u32[]{:S(2)}, u32[]{:S(2)}) async-start(f32[128,1,128]{2,1,0:T(1,128)} %stack.322), calls=%async_computation | async-start | bytes 131072 | tf_op jit(solution)/shard_map/all_to_all | solution.py:11
  40.0 0.9 fusion.83
  42.5 1.6 fusion.334
  44.8 302.1 %all-gather = f32[1,8,16384]{2,1,0:T(8,128)S(1)} all-gather(f32[1,8,128]{2,1,0:T(8,128)} %param.33), channel_id=2, replica_groups=mesh['shot'=4,'slab'=128] {'slab'}, dimensions={2}, use_global_device_ids=true | all-gather | bytes 528384 | tf_op jit(solution)/shard_map/all_gather | solution.py:133
  346.9 1.3 broadcast_select_fusion.1
  348.2 1.3 broadcast_select_fusion.6
  349.5 1.8 broadcast_select_fusion.4
  351.3 1.9 broadcast_select_fusion.2
  353.2 1.3 broadcast_select_fusion
  354.4 0.9 fusion.65
  355.5 1.3 collective-permute-start.1
  357.0 1.3 collective-permute-start.4
  359.0 4.5 collective-permute-done.4
  363.6 3.3 collective-permute-start.6
  367.0 1.3 collective-permute-done.6
  368.4 5.3 copy.267
  373.8 115.0 %scatter_custom_fusion = f32[8,8192]{0,1:T(8,128)} fusion(s32[16384]{0:T(1024)S(1)} %bitcast.953, f32[16384,8]{1,0:T(8,128)} %copy.267, f32[]{:T(128)} %constant.207.clone.1), kind=kCustom, calls=%fused_computation.9 | custom fusion | flops 131072 | bytes 262656 | tf_op jit(solution)/shard_map/scatter-add | solution.py:140
  488.8 28.8 %slice_reduce_fusion = (f32[8192]{0:T(1024)}, f32[8192]{0:T(1024)S(1)}, f32[8192]{0:T(1024)S(1)}, f32[8192]{0:T(1024)S(1)}, f32[8192]{0:T(1024)S(1)}, /*index=5*...) fusion(f32[8,8192]{0,1:T(8,128)} %scatter_custom_fusion), kind=kLoop, calls=%fused_computation.1 | loop fusion | bytes 524288 | tf_op jit(solution)/shard_map/slice | solution.py:170
  517.6 1.3 collective-permute-start.3
  519.2 1.3 collective-permute-start.8
  520.6 3.7 collective-permute-done.3
  524.3 5.8 collective-permute-start.5
  530.2 0.9 collective-permute-done.5
  531.3 1.3 collective-permute-start.7
  532.7 5.8 collective-permute-start.10
  538.7 5.8 collective-permute-start.9
  544.8 1.3 collective-permute-start.12
  546.1 5.2 collective-permute-done.12
  551.5 1.3 collective-permute-start.11
  552.9 5.5 collective-permute-start.14
  558.6 4.7 collective-permute-start.13
  563.6 1.3 collective-permute-start.16
  565.0 5.2 collective-permute-done.16
  570.3 1.3 collective-permute-start.15
  571.8 5.5 collective-permute-start.18
  577.4 4.9 collective-permute-start.17
  582.4 1.3 collective-permute-start.20
  584.0 5.0 collective-permute-done.20
  589.9 4.3 collective-permute-start.22
  594.9 1.3 collective-permute-start.19
  596.3 4.8 collective-permute-done.19
  601.3 1.3 collective-permute-start.24
  602.6 5.5 collective-permute-start.21
  609.1 0.8 multiply_subtract_fusion.4
  610.0 5.3 collective-permute-start.26
  615.5 1.3 collective-permute-start.23
  616.8 5.9 collective-permute-done.23
  622.9 1.3 collective-permute-start.28
  624.2 5.9 collective-permute-start.25
  632.1 1.3 collective-permute-start.27
  633.4 6.4 collective-permute-start.29
  641.3 6.0 collective-permute-start.30
  649.5 1.3 collective-permute-start.31
  652.3 4.6 collective-permute-done.31
  656.9 0.9 bitcast_dynamic-update-slice_fusion.2
  657.8 0.9 bitcast_dynamic-update-slice_fusion.1
  658.7 0.9 bitcast_dynamic-update-slice_fusion
  659.6 2.1 fusion.241
  661.8 0.9 fusion.4
  663.4 136.2 %reduce-scatter.3.cloned.1.call-done = f32[2,8,128]{2,1,0:T(8,128)} async-done(((f32[2,32,128]{2,1,0:T(8,128)}), f32[2,8,128]{2,1,0:T(8,128)}) %reduce-scatter.3.cloned.1.call-update) | async-done | bytes 8208 | tf_op jit(solution)/shard_map/reduce_scatter | solution.py:174
  799.6 28.9 %reduce-scatter.5.cloned.1.call-done = f32[2,8,128]{2,1,0:T(8,128)} async-done(((f32[2,32,128]{2,1,0:T(8,128)}), f32[2,8,128]{2,1,0:T(8,128)}) %reduce-scatter.5.cloned.1.call-update) | async-done | bytes 8208 | tf_op jit(solution)/shard_map/reduce_scatter | solution.py:175
  (199 shorter events, 18.8 us)
Async XLA Ops:
  7.2 348.2 %copy-start = (f32[1,9,2,32,128]{4,3,2,1,0:T(8,128)S(1)}, f32[1,9,2,32,128]{4,3,2,1,0:T(8,128)}, u32[]{:S(2)}) copy-start(f32[1,9,2,32,128]{4,3,2,1,0:T(8,128)} %param.29) | copy-start | bytes 884740
  7.2 348.2 %copy-start.1 = (f32[1,9,2,32,128]{4,3,2,1,0:T(8,128)S(1)}, f32[1,9,2,32,128]{4,3,2,1,0:T(8,128)}, u32[]{:S(2)}) copy-start(f32[1,9,2,32,128]{4,3,2,1,0:T(8,128)} %param.30) | copy-start | bytes 884740
  7.2 351.2 %copy-start.2 = (f32[2,32,128]{2,1,0:T(8,128)S(1)}, f32[2,32,128]{2,1,0:T(8,128)}, u32[]{:S(2)}) copy-start(f32[2,32,128]{2,1,0:T(8,128)} %param.26) | copy-start | bytes 98308
  8.1 355.5 %copy-start.3 = (f32[2,32,128]{2,1,0:T(8,128)S(1)}, f32[2,32,128]{2,1,0:T(8,128)}, u32[]{:S(2)}) copy-start(f32[2,32,128]{2,1,0:T(8,128)} %param.27) | copy-start | bytes 98308
  8.1 346.3 %collective-permute-start.2 = (f32[2,2,1,32,128]{4,3,0,2,1:T(8,128)S(1)}, f32[2,2,1,32,128]{4,3,0,2,1:T(8,128)S(1)}, u32[]{:S(2)}, u32[]{:S(2)}) collective-permute-start(f32[2,2,1,32,128]{4,3,0,2,1:T(8,128)S(1)} %get-tuple-element.218), channel_id=1, source_target_pairs={{0,1},{1,2},{2,3},{3,4},{4,5},{5,6},{6,7},{7,8},{8,9},{9,10},{10,1... | collective-permute-start | bytes 196616 | tf_op jit(solution)/shard_map/ppermute | solution.py:17
  14.4 341.0 %collective-permute-start = (f32[2,1,32,128]{3,2,0,1:T(8,128)S(1)}, f32[2,1,32,128]{3,2,0,1:T(8,128)S(1)}, u32[]{:S(2)}, u32[]{:S(2)}) collective-permute-start(f32[2,1,32,128]{3,2,0,1:T(8,128)S(1)} %get-tuple-element.213), channel_id=1, source_target_pairs={{1,0},{2,1},{3,2},{4,3},{5,4},{6,5},{7,6},{8,7},{9,8},{10,9},{11,1... | collective-permute-start | bytes 98312 | tf_op jit(solution)/shard_map/ppermute | solution.py:17
  17.0 351.3 %all-to-all-start = ((f32[128,1,128]{2,1,0:T(1,128)}), f32[128,1,128]{2,1,0:T(1,128)S(1)}, u32[]{:S(2)}, u32[]{:S(2)}) async-start(f32[128,1,128]{2,1,0:T(1,128)} %stack.322), calls=%async_computation | async-start | bytes 131072 | tf_op jit(solution)/shard_map/all_to_all | solution.py:11
  40.0 759.7 %reduce-scatter.3.cloned.1.call-start = ((), (), s32[]{:S(2)}) async-start(), calls=%async_computation.3 | async-start | bytes 40960 | tf_op jit(solution)/shard_map/reduce_scatter | solution.py:174
  355.5 2.8 collective-permute-start.1
  357.0 6.5 collective-permute-start.4
  363.6 4.6 collective-permute-start.6
  517.6 6.6 collective-permute-start.3
  519.2 11.9 %collective-permute-start.8 = (f32[2,2,1,32,128]{4,3,0,2,1:T(8,128)S(1)}, f32[2,2,1,32,128]{4,3,0,2,1:T(8,128)S(1)}, u32[]{:S(2)}, u32[]{:S(2)}) collective-permute-start(f32[2,2,1,32,128]{4,3,0,2,1:T(8,128)S(1)} %get-tuple-element.330), channel_id=1, source_target_pairs={{1,0},{2,1},{3,2},{4,3},{5,4},{6,5},{7,6},{8,7},{9,8},{10,9},{11,1... | collective-permute-start | bytes 196616 | tf_op jit(solution)/shard_map/ppermute | solution.py:17
  524.3 6.8 collective-permute-start.5
  531.3 7.2 collective-permute-start.7
  532.7 11.8 %collective-permute-start.10 = (f32[2,2,1,32,128]{4,3,0,2,1:T(8,128)S(1)}, f32[2,2,1,32,128]{4,3,0,2,1:T(8,128)S(1)}, u32[]{:S(2)}, u32[]{:S(2)}) collective-permute-start(f32[2,2,1,32,128]{4,3,0,2,1:T(8,128)S(1)} %fusion.47), channel_id=1, source_target_pairs={{0,1},{1,2},{2,3},{3,4},{4,5},{5,6},{6,7},{7,8},{8,9},{9,10},{10,1... | collective-permute-start | bytes 196616 | tf_op jit(solution)/shard_map/ppermute | solution.py:17
  538.7 7.4 collective-permute-start.9
  544.8 6.5 collective-permute-start.12
  551.3 19.0 %copy-start.6 = (f32[1,2,32,128]{3,2,1,0:T(8,128)S(1)}, f32[1,2,32,128]{3,2,1,0:T(8,128)}, u32[]{:S(2)}) copy-start(f32[1,2,32,128]{3,2,1,0:T(8,128)} %get-tuple-element.369) | copy-start | bytes 98308
  551.5 6.9 collective-permute-start.11
  552.9 10.5 %collective-permute-start.14 = (f32[2,2,1,32,128]{4,3,0,2,1:T(8,128)S(1)}, f32[2,2,1,32,128]{4,3,0,2,1:T(8,128)S(1)}, u32[]{:S(2)}, u32[]{:S(2)}) collective-permute-start(f32[2,2,1,32,128]{4,3,0,2,1:T(8,128)S(1)} %fusion.41), channel_id=1, source_target_pairs={{0,1},{1,2},{2,3},{3,4},{4,5},{5,6},{6,7},{7,8},{8,9},{9,10},{10,1... | collective-permute-start | bytes 196616 | tf_op jit(solution)/shard_map/ppermute | solution.py:17
  558.5 25.2 %copy-start.8 = (f32[1,2,32,128]{3,2,1,0:T(8,128)S(1)}, f32[1,2,32,128]{3,2,1,0:T(8,128)}, u32[]{:S(2)}) copy-start(f32[1,2,32,128]{3,2,1,0:T(8,128)} %broadcast_select_fusion.1) | copy-start | bytes 98308
  558.6 6.3 collective-permute-start.13
  563.6 6.5 collective-permute-start.16
  570.1 19.6 %copy-start.5 = (f32[1,2,32,128]{3,2,1,0:T(8,128)S(1)}, f32[1,2,32,128]{3,2,1,0:T(8,128)}, u32[]{:S(2)}) copy-start(f32[1,2,32,128]{3,2,1,0:T(8,128)} %get-tuple-element.368) | copy-start | bytes 98308
  570.3 6.9 collective-permute-start.15
  571.8 10.5 %collective-permute-start.18 = (f32[2,2,1,32,128]{4,3,0,2,1:T(8,128)S(1)}, f32[2,2,1,32,128]{4,3,0,2,1:T(8,128)S(1)}, u32[]{:S(2)}, u32[]{:S(2)}) collective-permute-start(f32[2,2,1,32,128]{4,3,0,2,1:T(8,128)S(1)} %fusion.35), channel_id=1, source_target_pairs={{0,1},{1,2},{2,3},{3,4},{4,5},{5,6},{6,7},{7,8},{8,9},{9,10},{10,1... | collective-permute-start | bytes 196616 | tf_op jit(solution)/shard_map/ppermute | solution.py:17
  577.4 6.6 collective-permute-start.17
  582.3 25.8 %copy-start.7 = (f32[1,2,32,128]{3,2,1,0:T(8,128)S(1)}, f32[1,2,32,128]{3,2,1,0:T(8,128)}, u32[]{:S(2)}) copy-start(f32[1,2,32,128]{3,2,1,0:T(8,128)} %broadcast_select_fusion) | copy-start | bytes 98308
  582.3 25.8 %copy-start.9 = (f32[8192]{0:T(1024)S(1)}, f32[8192]{0:T(1024)}, u32[]{:S(2)}) copy-start(f32[8192]{0:T(1024)} %get-tuple-element.108) | copy-start | bytes 98308
  582.4 6.5 collective-permute-start.20
  589.9 6.4 collective-permute-start.22
  594.9 6.2 collective-permute-start.19
  601.3 7.8 collective-permute-start.24
  602.6 6.5 collective-permute-start.21
  610.0 6.7 collective-permute-start.26
  615.5 7.2 collective-permute-start.23
  622.9 8.3 collective-permute-start.28
  624.2 7.0 collective-permute-start.25
  632.1 7.8 collective-permute-start.27
  633.4 14.0 %collective-permute-start.29 = (f32[2,2,1,32,128]{4,3,2,0,1:T(8,128)S(1)}, f32[2,2,1,32,128]{4,3,2,0,1:T(8,128)S(1)}, u32[]{:S(2)}, u32[]{:S(2)}) collective-permute-start(f32[2,2,1,32,128]{4,3,2,0,1:T(8,128)S(1)} %fusion.17), channel_id=1, source_target_pairs={{0,1},{1,2},{2,3},{3,4},{4,5},{5,6},{6,7},{7,8},{8,9},{9,10},{10,1... | collective-permute-start | bytes 196616 | tf_op jit(solution)/shard_map/ppermute | solution.py:17
  641.3 9.5 %collective-permute-start.30 = (f32[2,1,1,32,128]{4,3,2,0,1:T(8,128)S(1)}, f32[2,1,1,32,128]{4,3,2,0,1:T(8,128)S(1)}, u32[]{:S(2)}, u32[]{:S(2)}) collective-permute-start(f32[2,1,1,32,128]{4,3,2,0,1:T(8,128)S(1)} %get-tuple-element.340), channel_id=1, source_target_pairs={{0,1},{1,2},{2,3},{3,4},{4,5},{5,6},{6,7},{7,8},{8,9},{9,10},{10,1... | collective-permute-start | bytes 98312 | tf_op jit(solution)/shard_map/ppermute | solution.py:17
  649.5 7.4 collective-permute-start.31
  651.6 177.0 %reduce-scatter.5.cloned.1.call-start = ((), (), s32[]{:S(2)}) async-start(), calls=%async_computation.4 | async-start | bytes 40960 | tf_op jit(solution)/shard_map/reduce_scatter | solution.py:175
  652.3 9.5 %copy-start.4 = (f32[2,1,2,32,128]{4,3,2,0,1:T(8,128)S(1)}, f32[2,1,2,32,128]{4,3,2,0,1:T(8,128)}, u32[]{:S(2)}) copy-start(f32[2,1,2,32,128]{4,3,2,0,1:T(8,128)} %get-tuple-element.123) | copy-start | bytes 196612
Sparse Core Ops, SparseCore 0:
  651.7 147.8 reduce-scatter.2
  803.2 25.3 reduce-scatter.4
